TPU v7x, 256 devices: a whole 4x4x8 slice. The times are simulated.
256 devices in a mesh: ctx: 32 (over x, z_hi, y), exp: 8 (over z_lo, core).
Axes of the slice: x: 4, y: 4, z: 8 (z_hi: 2, z_lo: 4; z = z_hi * 4 + z_lo), core: 2. Of those that a mesh axis runs over, the one named last changes fastest.
Arguments:
- queries: bfloat16 [256, 32, 128], P(None, 'exp'), may hold values from -64 to 64
- keys: bfloat16 [32768, 8, 128], P('ctx', 'exp'), may hold values from -8 to 8
- values: bfloat16 [32768, 8, 128], P('ctx', 'exp'), may hold values from -32 to 32
- out_proj: bfloat16 [4096, 4096], P('exp', 'ctx'), may hold values from -0.09375 to 0.09375
- residual: bfloat16 [256, 4096], P('ctx'), may hold values from -6 to 6
- gain: float32 [4096], replicated, may hold values from 0.1 to 1.9
- routes: int32 [256, 2], P('ctx'), may hold values from 0 to 7, all different within a row; in each aligned block of 8 rows (0 to 7, 8 to 15, ...) at most 4 rows name the same one
- gates: float32 [256, 2], P('ctx'), may hold values from 0.25 to 1
- w_gate: bfloat16 [8, 4096, 14336], P('exp', None, 'ctx'), may hold values from -0.09375 to 0.09375
- w_up: bfloat16 [8, 4096, 14336], P('exp', None, 'ctx'), may hold values from -0.09375 to 0.09375
- w_down: bfloat16 [8, 14336, 4096], P('exp', 'ctx'), may hold values from -0.046875 to 0.046875
Outputs:
- mixed: bfloat16 [256, 4096], P('ctx', 'exp')
Inputs may be any that keep to these rules, and one draw needn't show every extreme that they name: `routes`: within each aligned block of 8 rows no expert is named by more than 4 rows, some expert is named by exactly 4 rows in some block, and the 2 experts of a row differ.
All inputs are finite; a program needn't handle non-finite values.
Results may differ from a plain program's by a relative error of at most 0.017.
Values may be sent and summed in bfloat16 or wider, within the bound.
A program may use at most 128 MiB of HBM per device.

v0:
```python
import math
import jax
import jax.numpy as jnp
from jax import lax
from jax.sharding import PartitionSpec as P


def joined(part, axis, combine):
    gathered = jax.tree.map(lambda a: lax.all_gather(a, axis), part)

    def take(source):
        return jax.tree.map(lambda a: lax.dynamic_index_in_dim(a, source, 0, False), gathered)

    return lax.fori_loop(
        1, lax.axis_size(axis), lambda source, state: combine(state, take(source)), take(0)
    )


def combine_parts(first_part, second_part):
    top_level = jnp.maximum(first_part[0], second_part[0])
    first_scale = jnp.exp(first_part[0] - top_level)
    second_scale = jnp.exp(second_part[0] - top_level)
    summed = first_part[1] * first_scale + second_part[1] * second_scale
    weighted = first_part[2] * first_scale[..., None] + second_part[2] * second_scale[..., None]
    return (top_level, summed, weighted)


def local(queries, keys, values, out_proj, residual, gain, routes, gates, w_gate, w_up, w_down):
    tokens_all, heads_local, head_dim = queries.shape
    key_rows, kv_local, unused_dim = keys.shape
    groups = heads_local // kv_local
    ctx_count = lax.axis_size("ctx")
    ctx_index = lax.axis_index("ctx")
    exp_index = lax.axis_index("exp")
    block_rows = residual.shape[0]
    total_len = key_rows * ctx_count
    score_scale = 1.0 / math.sqrt(head_dim)
    grouped = queries.reshape(tokens_all, kv_local, groups, head_dim)
    scores = (
        jnp.einsum("tgrd,sgd->gtrs", grouped, keys, preferred_element_type=jnp.float32)
        * score_scale
    )
    key_pos = ctx_index * key_rows + jnp.arange(key_rows, dtype=jnp.int32)
    query_pos = total_len - tokens_all + jnp.arange(tokens_all, dtype=jnp.int32)
    visible = (key_pos[None, :] <= query_pos[:, None])[None, :, None, :]
    scores = jnp.where(visible, scores, jnp.float32(-1e30))
    block_max = jnp.max(scores, axis=-1)
    expw = jnp.where(visible, jnp.exp(scores - block_max[..., None]), jnp.float32(0.0))
    block_sum = jnp.sum(expw, axis=-1)
    block_out = jnp.einsum(
        "gtrs,sgd->gtrd", expw.astype(jnp.bfloat16), values, preferred_element_type=jnp.float32
    )
    merged = joined((block_max, block_sum, block_out), "ctx", combine_parts)
    attended_all = merged[2] / merged[1][..., None]
    own_rows = lax.dynamic_slice_in_dim(attended_all, ctx_index * block_rows, block_rows, 1)
    attended = (
        own_rows.transpose(1, 0, 2, 3)
        .reshape(block_rows, heads_local * head_dim)
        .astype(jnp.bfloat16)
    )
    partial_value = jnp.dot(
        attended,
        lax.all_gather(out_proj, "ctx", axis=1, tiled=True),
        preferred_element_type=jnp.float32,
    )
    stream = residual.astype(jnp.float32) + lax.psum(
        partial_value.astype(jnp.bfloat16), "exp"
    ).astype(jnp.float32)
    normed = (
        stream * lax.rsqrt(jnp.mean(stream * stream, axis=-1, keepdims=True) + 1e-05) * gain
    ).astype(jnp.bfloat16)
    experts_local = w_gate.shape[0]
    expert_count = experts_local * lax.axis_size("exp")
    top_count = routes.shape[1]
    capacity = min(block_rows, 2 * top_count * block_rows // expert_count)
    flat_ids = routes.reshape(block_rows * top_count)
    onehot = (flat_ids[:, None] == jnp.arange(expert_count, dtype=jnp.int32)[None, :]).astype(
        jnp.int32
    )
    before = jnp.cumsum(onehot, axis=0, dtype=jnp.int32) - onehot
    slot_of = jnp.sum(before * onehot, axis=1, dtype=jnp.int32)
    mine_ids = exp_index * experts_local + jnp.arange(experts_local, dtype=jnp.int32)
    is_mine = flat_ids[:, None] == mine_ids[None, :]
    slot_hit = is_mine[:, :, None] & (
        slot_of[:, None, None] == jnp.arange(capacity, dtype=jnp.int32)[None, None, :]
    )
    slot_hit = slot_hit.astype(jnp.float32).reshape(block_rows, top_count, experts_local, capacity)
    dispatch_map = jnp.sum(slot_hit, axis=1)
    combine_map = jnp.sum(slot_hit * gates[:, :, None, None], axis=1)
    buffer = jnp.einsum(
        "tec,td->ced", dispatch_map.astype(jnp.bfloat16), normed, preferred_element_type=jnp.float32
    ).astype(jnp.bfloat16)
    shard_rows = lax.all_gather(buffer, "ctx", axis=0, tiled=True)
    gate_val = jnp.einsum("ned,edf->nef", shard_rows, w_gate, preferred_element_type=jnp.float32)
    up_val = jnp.einsum("ned,edf->nef", shard_rows, w_up, preferred_element_type=jnp.float32)
    act = (jax.nn.silu(gate_val) * up_val).astype(jnp.bfloat16)
    expert_out = lax.psum_scatter(
        jnp.einsum("nef,efd->ned", act, w_down, preferred_element_type=jnp.float32).astype(
            jnp.bfloat16
        ),
        "ctx",
        scatter_dimension=0,
        tiled=True,
    ).astype(jnp.float32)
    contribution = jnp.einsum(
        "tec,ced->td", combine_map, expert_out, precision=lax.Precision.HIGHEST
    )
    moe_share = lax.psum_scatter(
        contribution.astype(jnp.bfloat16), "exp", scatter_dimension=1, tiled=True
    ).astype(jnp.float32)
    feat_width = moe_share.shape[1]
    own_stream = lax.dynamic_slice_in_dim(stream, exp_index * feat_width, feat_width, 1)
    return (own_stream + moe_share).astype(jnp.bfloat16)


def solution(mesh):
    return jax.shard_map(
        local,
        mesh=mesh,
        in_specs=(
            P(None, "exp", None),
            P("ctx", "exp", None),
            P("ctx", "exp", None),
            P("exp", "ctx"),
            P("ctx", None),
            P(),
            P("ctx", None),
            P("ctx", None),
            P("exp", None, "ctx"),
            P("exp", None, "ctx"),
            P("exp", "ctx", None),
        ),
        out_specs=P("ctx", "exp"),
        check_vma=False,
    )
```

profile of v0, /device:TPU:2, one launch (start us, length us, event | category | flops | bytes accessed | tf_op | source)
XLA Modules:
  0.0 1042.4 jit_solution(11815722336202214809)
XLA Ops:
  7.5 2.0 fusion.8
  9.5 2.0 copy-done.1
  11.4 2.2 fusion.16
  14.5 3.7 fusion.15
  18.1 112.5 %all-gather = f32[8192,4]{0,1:T(4,128)S(1)} all-gather(f32[256,4]{0,1:T(4,128)S(1)} %get-tuple-element.241), channel_id=2, replica_groups=mesh['ctx'=32,'exp'=8] {'ctx'}, dimensions={0}, use_global_device_ids=true | all-gather | bytes 135168 | tf_op jit(solution)/shard_map/all_gather | solution.py:9
  130.7 123.6 %all-gather.1 = f32[8192,4]{0,1:T(4,128)S(1)} all-gather(f32[256,4]{0,1:T(4,128)S(1)} %fusion.15), channel_id=3, replica_groups=mesh['ctx'=32,'exp'=8] {'ctx'}, dimensions={0}, use_global_device_ids=true | all-gather | bytes 135168 | tf_op jit(solution)/shard_map/all_gather | solution.py:9
  254.9 12.9 %all-gather.11.cloned.1.call-done = f32[8192,4,128]{2,0,1:T(8,128)} async-done(((f32[256,4,128]{2,0,1:T(8,128)}), f32[8192,4,128]{2,0,1:T(8,128)}) %all-gather.11.cloned.1.call-update) | async-done | bytes 16777232 | tf_op jit(solution)/shard_map/all_gather | solution.py:9
  269.3 84.7 %while.19 = (s32[]{:T(128)}, f32[1,256,4]{1,2,0:T(4,128)S(1)}, f32[1,256,4]{1,2,0:T(4,128)S(1)}, f32[1,256,4,128]{3,2,1,0:T(4,128)S(1)}, f32[32,1,256,4]{2,3,1,0...) while((s32[]{:T(128)}, f32[1,256,4]{1,2,0:T(4,128)S(1)}, ...), condition=%wide.region_3.4_spmd, body=%wide.region_2.3_spmd.sunk | while | flops 400389 | bytes 2699419 | solution.py:14
  270.8 1.3 fusion.75
  273.5 1.3 fusion.75
  279.0 1.3 fusion.75
  287.2 1.3 fusion.75
  292.6 1.3 fusion.75
  300.8 1.3 fusion.75
  309.0 1.3 fusion.75
  317.2 1.3 fusion.75
  325.4 1.3 fusion.75
  330.9 1.3 fusion.75
  333.6 1.3 fusion.75
  336.4 1.3 fusion.75
  344.5 1.3 fusion.75
  350.0 1.3 fusion.75
  354.3 45.0 %all-gather.7.cloned.1.call-done = bf16[512,4096]{1,0:T(8,128)(2,1)} async-done(((bf16[512,128]{1,0:T(8,128)(2,1)}), bf16[512,4096]{1,0:T(8,128)(2,1)}) %all-gather.7.cloned.1.call-update) | async-done | bytes 4194320 | tf_op jit(solution)/shard_map/all_gather | solution.py:63
  399.3 3.5 convolution_convert_fusion.2
  402.9 65.4 %all-reduce.4.cloned.1.call-done = bf16[8,4096]{1,0:T(8,128)(2,1)} async-done(((bf16[8,4096]{1,0:T(8,128)(2,1)}), bf16[8,4096]{1,0:T(8,128)(2,1)}) %all-reduce.4.cloned.1.call-update) | async-done | bytes 65552 | tf_op jit(solution)/shard_map/psum | solution.py:66
  471.1 90.5 %all-gather.9.cloned.1.call-done = bf16[128,1,4096]{2,1,0:T(2,128)(2,1)} async-done(((bf16[4,1,4096]{2,1,0:T(2,128)(2,1)}), bf16[128,1,4096]{2,1,0:T(2,128)(2,1)}) %all-gather.9.cloned.1.call-update) | async-done | bytes 1048592 | tf_op jit(solution)/shard_map/all_gather | solution.py:93
  561.6 4.8 fusion.19
  566.4 7.3 fusion.6
  574.9 405.6 %all-reduce.6.cloned.1.call-done = bf16[128,1,4096]{2,0,1:T(8,128)(2,1)} async-done(((bf16[128,1,4096]{2,0,1:T(8,128)(2,1)}), bf16[128,1,4096]{2,0,1:T(8,128)(2,1)}) %all-reduce.6.cloned.1.call-update) | async-done | bytes 1048592
  980.5 1.7 convolution_convert_fusion.1
  982.3 52.0 %reduce-scatter.3.cloned.1.call-done = bf16[8,512]{1,0:T(8,128)(2,1)} async-done(((bf16[8,4096]{1,0:T(8,128)(2,1)}), bf16[8,512]{1,0:T(8,128)(2,1)}) %reduce-scatter.3.cloned.1.call-update) | async-done | bytes 8208 | tf_op jit(solution)/shard_map/reduce_scatter | solution.py:108
  1034.3 1.3 add_convert_fusion
  (256 shorter events, 72.5 us)
Async XLA Ops:
  6.5 1.0 copy-start
  6.5 4.9 copy-start.7
  6.5 261.3 %all-gather.11.cloned.1.call-start = ((), (), s32[]{:S(2)}) async-start(), calls=%async_computation.5 | async-start | bytes 17301504 | tf_op jit(solution)/shard_map/all_gather | solution.py:9
  9.4 2.0 copy-start.1
  13.6 240.7 %copy-start.5 = (s32[8,2]{0,1:T(2,128)S(1)}, s32[8,2]{0,1:T(2,128)}, u32[]{:S(2)}) copy-start(s32[8,2]{0,1:T(2,128)} %param.19) | copy-start | bytes 196
  13.7 385.6 %all-gather.7.cloned.1.call-start = ((), (), s32[]{:S(2)}) async-start(), calls=%async_computation.1 | async-start | bytes 4325376 | tf_op jit(solution)/shard_map/all_gather | solution.py:63
  14.4 453.8 %all-reduce.4.cloned.1.call-start = ((), (), s32[]{:S(2)}) async-start(), calls=%async_computation.2 | async-start | bytes 131072 | tf_op jit(solution)/shard_map/psum | solution.py:66
  354.0 48.8 %copy-start.6 = (f32[8,2]{0,1:T(2,128)S(1)}, f32[8,2]{0,1:T(2,128)}, u32[]{:S(2)}) copy-start(f32[8,2]{0,1:T(2,128)} %param.20) | copy-start | bytes 196
  354.0 114.2 %copy-start.3 = (bf16[8,4096]{1,0:T(8,128)(2,1)S(1)}, bf16[8,4096]{1,0:T(8,128)(2,1)}, u32[]{:S(2)}) copy-start(bf16[8,4096]{1,0:T(8,128)(2,1)} %param.17) | copy-start | bytes 196612
  354.1 115.2 %copy-start.4 = (f32[4096]{0:T(1024)S(1)}, f32[4096]{0:T(1024)}, u32[]{:S(2)}) copy-start(f32[4096]{0:T(1024)} %param.18) | copy-start | bytes 49156
  402.8 158.8 %all-gather.9.cloned.1.call-start = ((), (), s32[]{:S(2)}) async-start(), calls=%async_computation.3 | async-start | bytes 2162688 | tf_op jit(solution)/shard_map/all_gather | solution.py:93
  471.0 509.5 %all-reduce.6.cloned.1.call-start = ((), (), s32[]{:S(2)}) async-start(), calls=%async_computation.6 | async-start | bytes 2097152
  561.6 4.8 copy-start.2
  566.3 7.4 copy-start.8
  573.6 460.6 %reduce-scatter.3.cloned.1.call-start = ((), (), s32[]{:S(2)}) async-start(), calls=%async_computation.4 | async-start | bytes 73728 | tf_op jit(solution)/shard_map/reduce_scatter | solution.py:108
Sparse Core Ops, SparseCore 0:
  13.8 254.0 all-gather.10
  271.1 128.1 all-gather.6
  402.9 65.3 all-reduce.3
  472.2 89.3 all-gather.8
  573.8 406.6 all-reduce.5
  982.9 51.3 reduce-scatter.2
where the time goes:
time: 1040 us
  waiting for transfers between devices  672 us (65%)
  blocking collectives  236 us (23%)
  local copies, waits for them, and re-layouts  48.1 us (5%)
  other arithmetic  47.1 us (5%)
  matrix products  22.4 us (2%)
  between operations  14.3 us (1%)
    unnamed x7, waiting for transfers between devices  406 us
    all_gather x2, blocking collectives, joined(): gathered = jax.tree.map(lambda a: lax.all_gather(a, axis), part)  236 us
    all_gather x1, waiting for transfers between devices, local(): shard_rows = lax.all_gather(buffer, 'ctx', axis=0, tiled=True)  90.5 us
    psum x1, waiting for transfers between devices, local(): lax.psum(partial_value.astype(jnp.bfloat16), 'exp').astype(jnp.float32)  65.4 us
    reduce_scatter x1, waiting for transfers between devices, local(): lax.psum_scatter(contribution.astype(jnp.bfloat16), 'exp', scatter_dimens...  52 us
    all_gather x1, waiting for transfers between devices, local(): lax.all_gather(out_proj, 'ctx', axis=1, tiled=True)  45 us
    add x31, other arithmetic, combine_parts(): first_part[2] * first_scale[..., None]  39.3 us
    dynamic_slice x31, local copies, waits for them, and re-layouts, take(): lax.dynamic_index_in_dim(a, source, 0, False)  33.8 us
  transfers between devices with their start and end apart: 6, of which 6 were waited for; matrix products, arithmetic and copies ran while one was open for 9% of the time, Pallas kernels for 0%

commit v1 on v0

--- a/solution.py
+++ b/solution.py
@@ -63,8 +63,8 @@
         lax.all_gather(out_proj, "ctx", axis=1, tiled=True),
         preferred_element_type=jnp.float32,
     )
-    stream = residual.astype(jnp.float32) + lax.psum(
-        partial_value.astype(jnp.bfloat16), "exp"
+    stream = residual.astype(jnp.float32) + jnp.sum(
+        lax.all_gather(partial_value.astype(jnp.bfloat16), "exp"), axis=0
     ).astype(jnp.float32)
     normed = (
         stream * lax.rsqrt(jnp.mean(stream * stream, axis=-1, keepdims=True) + 1e-05) * gain

time: 1040 us -> 988 us (0.950)
  waiting for transfers between devices: 672 us -> 603 us
  blocking collectives: 236 us -> 251 us
    psum x1 -> x0, waiting for transfers between devices: 65.4 us -> none  [local(): lax.psum(partial_value.astype(jnp.bfloat16), 'exp').astype(jnp.float32)]
    all_gather x0 -> x1, blocking collectives: none -> 14.9 us  [local(): lax.all_gather(partial_value.astype(jnp.bfloat16), 'exp')]
    unnamed x7 -> x6, waiting for transfers between devices: 406 us -> 406 us
  transfers between devices with their start and end apart: 6 -> 5, of which waited for: 6 -> 5; matrix products, arithmetic and copies ran while one was open for 9% -> 9% of each run, Pallas kernels for 0% -> 0%
where the time goes in v1:
time: 988 us; the launch traced here: 986 us
  waiting for transfers between devices  603 us (61%)
  blocking collectives  251 us (25%)
  local copies, waits for them, and re-layouts  48.1 us (5%)
  other arithmetic  46.3 us (5%)
  matrix products  21 us (2%)
  between operations  14 us (1%)
    unnamed x6, waiting for transfers between devices  406 us
    all_gather x2, blocking collectives, joined(): gathered = jax.tree.map(lambda a: lax.all_gather(a, axis), part)  236 us
    all_gather x1, waiting for transfers between devices, local(): shard_rows = lax.all_gather(buffer, 'ctx', axis=0, tiled=True)  86.5 us
    reduce_scatter x1, waiting for transfers between devices, local(): lax.psum_scatter(contribution.astype(jnp.bfloat16), 'exp', scatter_dimens...  52.2 us
    all_gather x1, waiting for transfers between devices, local(): lax.all_gather(out_proj, 'ctx', axis=1, tiled=True)  45 us
    add x31, other arithmetic, combine_parts(): first_part[2] * first_scale[..., None]  39.3 us
    dynamic_slice x31, local copies, waits for them, and re-layouts, take(): lax.dynamic_index_in_dim(a, source, 0, False)  33.8 us
  transfers between devices with their start and end apart: 5, of which 5 were waited for; matrix products, arithmetic and copies ran while one was open for 9% of the time, Pallas kernels for 0%

profile of v1, /device:TPU:2, one launch (start us, length us, event | category | flops | bytes accessed | tf_op | source)
XLA Modules:
  0.0 985.8 jit_solution(14726933974939099324)
XLA Ops:
  7.5 2.0 fusion.8
  9.5 2.0 copy-done.1
  11.4 2.2 fusion.16
  14.5 3.7 fusion.15
  18.1 112.6 %all-gather = f32[8192,4]{0,1:T(4,128)S(1)} all-gather(f32[256,4]{0,1:T(4,128)S(1)} %get-tuple-element.241), channel_id=2, replica_groups=mesh['ctx'=32,'exp'=8] {'ctx'}, dimensions={0}, use_global_device_ids=true | all-gather | bytes 135168 | tf_op jit(solution)/shard_map/all_gather | solution.py:9
  130.7 123.6 %all-gather.1 = f32[8192,4]{0,1:T(4,128)S(1)} all-gather(f32[256,4]{0,1:T(4,128)S(1)} %fusion.15), channel_id=3, replica_groups=mesh['ctx'=32,'exp'=8] {'ctx'}, dimensions={0}, use_global_device_ids=true | all-gather | bytes 135168 | tf_op jit(solution)/shard_map/all_gather | solution.py:9
  254.9 13.0 %all-gather.12.cloned.1.call-done = f32[8192,4,128]{2,0,1:T(8,128)} async-done(((f32[256,4,128]{2,0,1:T(8,128)}), f32[8192,4,128]{2,0,1:T(8,128)}) %all-gather.12.cloned.1.call-update) | async-done | bytes 16777232 | tf_op jit(solution)/shard_map/all_gather | solution.py:9
  269.3 84.7 %while.19 = (s32[]{:T(128)}, f32[1,256,4]{1,2,0:T(4,128)S(1)}, f32[1,256,4]{1,2,0:T(4,128)S(1)}, f32[1,256,4,128]{3,2,1,0:T(4,128)S(1)}, f32[32,1,256,4]{2,3,1,0...) while((s32[]{:T(128)}, f32[1,256,4]{1,2,0:T(4,128)S(1)}, ...), condition=%wide.region_3.4_spmd, body=%wide.region_2.3_spmd.sunk | while | flops 400389 | bytes 2699419 | solution.py:14
  270.8 1.3 fusion.75
  273.5 1.3 fusion.75
  281.7 1.3 fusion.75
  284.4 1.3 fusion.75
  289.9 1.3 fusion.75
  298.1 1.3 fusion.75
  306.3 1.3 fusion.75
  314.5 1.3 fusion.75
  319.9 1.3 fusion.75
  322.7 1.3 fusion.75
  328.1 1.3 fusion.75
  339.1 1.3 fusion.75
  341.8 1.3 fusion.75
  347.3 1.3 fusion.75
  354.3 45.0 %all-gather.8.cloned.1.call-done = bf16[512,4096]{1,0:T(8,128)(2,1)} async-done(((bf16[512,128]{1,0:T(8,128)(2,1)}), bf16[512,4096]{1,0:T(8,128)(2,1)}) %all-gather.8.cloned.1.call-update) | async-done | bytes 4194320 | tf_op jit(solution)/shard_map/all_gather | solution.py:63
  399.3 2.8 convolution_convert_fusion.2
  402.1 14.9 %all-gather.3 = bf16[64,4096]{1,0:T(8,128)(2,1)S(1)} all-gather(bf16[8,4096]{1,0:T(8,128)(2,1)S(1)} %convolution_convert_fusion.2), channel_id=5, replica_groups=mesh['ctx'=32,'exp'=8] {'exp'}, dimensions={0}, use_global_device_ids=true | all-gather | bytes 589824 | tf_op jit(solution)/shard_map/all_gather | solution.py:67
  418.5 86.5 %all-gather.10.cloned.1.call-done = bf16[128,1,4096]{2,1,0:T(2,128)(2,1)} async-done(((bf16[4,1,4096]{2,1,0:T(2,128)(2,1)}), bf16[128,1,4096]{2,1,0:T(2,128)(2,1)}) %all-gather.10.cloned.1.call-update) | async-done | bytes 1048592 | tf_op jit(solution)/shard_map/all_gather | solution.py:93
  505.0 4.8 fusion.19
  509.8 7.3 fusion.6
  518.4 405.6 %all-reduce.3.cloned.1.call-done = bf16[128,1,4096]{2,0,1:T(8,128)(2,1)} async-done(((bf16[128,1,4096]{2,0,1:T(8,128)(2,1)}), bf16[128,1,4096]{2,0,1:T(8,128)(2,1)}) %all-reduce.3.cloned.1.call-update) | async-done | bytes 1048592
  924.1 1.7 convolution_convert_fusion.1
  925.8 52.2 %reduce-scatter.3.cloned.1.call-done = bf16[8,512]{1,0:T(8,128)(2,1)} async-done(((bf16[8,4096]{1,0:T(8,128)(2,1)}), bf16[8,512]{1,0:T(8,128)(2,1)}) %reduce-scatter.3.cloned.1.call-update) | async-done | bytes 8208 | tf_op jit(solution)/shard_map/reduce_scatter | solution.py:108
  978.0 1.3 add_convert_fusion
  (255 shorter events, 71.1 us)
Async XLA Ops:
  6.5 1.0 copy-start
  6.5 4.9 copy-start.7
  6.5 261.4 %all-gather.12.cloned.1.call-start = ((), (), s32[]{:S(2)}) async-start(), calls=%async_computation.4 | async-start | bytes 17301504 | tf_op jit(solution)/shard_map/all_gather | solution.py:9
  9.4 2.0 copy-start.1
  13.6 240.6 %copy-start.5 = (s32[8,2]{0,1:T(2,128)S(1)}, s32[8,2]{0,1:T(2,128)}, u32[]{:S(2)}) copy-start(s32[8,2]{0,1:T(2,128)} %param.19) | copy-start | bytes 196
  13.6 241.2 %copy-start.6 = (f32[8,2]{0,1:T(2,128)S(1)}, f32[8,2]{0,1:T(2,128)}, u32[]{:S(2)}) copy-start(f32[8,2]{0,1:T(2,128)} %param.20) | copy-start | bytes 196
  13.7 385.6 %all-gather.8.cloned.1.call-start = ((), (), s32[]{:S(2)}) async-start(), calls=%async_computation.1 | async-start | bytes 4325376 | tf_op jit(solution)/shard_map/all_gather | solution.py:63
  14.4 490.6 %all-gather.10.cloned.1.call-start = ((), (), s32[]{:S(2)}) async-start(), calls=%async_computation.2 | async-start | bytes 2162688 | tf_op jit(solution)/shard_map/all_gather | solution.py:93
  354.0 63.1 %copy-start.3 = (bf16[8,4096]{1,0:T(8,128)(2,1)S(1)}, bf16[8,4096]{1,0:T(8,128)(2,1)}, u32[]{:S(2)}) copy-start(bf16[8,4096]{1,0:T(8,128)(2,1)} %param.17) | copy-start | bytes 196612
  354.1 63.3 %copy-start.4 = (f32[4096]{0:T(1024)S(1)}, f32[4096]{0:T(1024)}, u32[]{:S(2)}) copy-start(f32[4096]{0:T(1024)} %param.18) | copy-start | bytes 49156
  418.2 505.8 %all-reduce.3.cloned.1.call-start = ((), (), s32[]{:S(2)}) async-start(), calls=%async_computation.5 | async-start | bytes 2097152
  505.0 4.8 copy-start.2
  509.8 7.4 copy-start.8
  517.1 460.9 %reduce-scatter.3.cloned.1.call-start = ((), (), s32[]{:S(2)}) async-start(), calls=%async_computation.3 | async-start | bytes 73728 | tf_op jit(solution)/shard_map/reduce_scatter | solution.py:108
Sparse Core Ops, SparseCore 0:
  13.8 254.0 all-gather.11
  271.1 128.1 all-gather.7
  418.4 86.5 all-gather.9
  517.3 406.7 all-reduce.2
  926.6 51.3 reduce-scatter.2
